TPU v7x, 256 devices: a whole 4x4x8 slice. The times are simulated.
256 devices in a mesh: row: 8 (over x, core), col: 32 (over y, z).
Axes of the slice: x: 4, y: 4, z: 8, core: 2. Of those that a mesh axis runs over, the one named last changes fastest.
Arguments:
- frames: bfloat16 [3072, 4096], P('row', 'col'), may hold values from -6 to 6
- gain: float32 [4096], replicated, may hold values from 0.3 to 10
- w_value: bfloat16 [4096, 4096], P('row', 'col'), may hold values from -0.09375 to 0.09375
- w_gate: bfloat16 [4096, 4096], P('row', 'col'), may hold values from -0.09375 to 0.09375
- kernel: float32 [31, 4096], P(None, 'col'), may hold values from -1.5 to 1.5
- bias: float32 [4096], P('col'), may hold values from -3 to 3
- w_out: bfloat16 [4096, 4096], P('row', 'col'), may hold values from -0.09375 to 0.09375
- grad_out: bfloat16 [3072, 4096], P('row', 'col'), may hold values from -6 to 6
Outputs:
- encoded: bfloat16 [3072, 4096], P('row', 'col')
- input_grad: bfloat16 [3072, 4096], P('row', 'col')
- grad_value: float32 [4096, 4096], P('row', 'col')
- grad_gate: float32 [4096, 4096], P('row', 'col')
- grad_kernel: float32 [31, 4096], P(None, 'col')
- grad_bias: float32 [4096], P('col')
- grad_out_weight: float32 [4096, 4096], P('row', 'col')
- grad_gain: float32 [4096], P('col')
All inputs are finite; a program needn't handle non-finite values.
Results may differ from a plain program's by a relative error of at most 0.035.
Values may be sent and summed in bfloat16 or wider, within the bound.
No kernel may reach another device: no remote copies, remote signals or barrier semaphores. Data moves between devices by JAX's collectives and lax.ppermute only.
A program may use at most 128 MiB of HBM per device.

v0:
```python
import jax
import jax.numpy as jnp
from jax import lax
from jax.sharding import PartitionSpec as P

K = 31
LEN = 2048
epsilon = 1e-05


def extended(block, sides, width):
    for axis, dim in sides:
        count = lax.axis_size(axis)
        forward = [(i, i + 1) for i in range(count - 1)]
        backward = [(target, source) for source, target in forward]
        low = lax.ppermute(
            lax.slice_in_dim(block, block.shape[dim] - width, None, axis=dim), axis, forward
        )
        high = lax.ppermute(lax.slice_in_dim(block, 0, width, axis=dim), axis, backward)
        block = jnp.concatenate([low, block, high], axis=dim)
    return block


def tap_masks(positions):
    offsets = jnp.arange(K, dtype=jnp.int32) - K // 2
    placed = (positions % LEN)[None, :] + offsets[:, None]
    return ((placed >= 0) & (placed < LEN)).astype(jnp.float32)


def contract_rows(left, right):
    return lax.dot_general(
        left, right, (((0,), (0,)), ((), ())), preferred_element_type=jnp.float32
    )


def contract_cols(left, right):
    return lax.dot_general(
        left, right, (((1,), (1,)), ((), ())), preferred_element_type=jnp.float32
    )


def shards(frames, gain, w_value, w_gate, kernel, bias, w_out, grad_out):
    row_count = frames.shape[0]
    col_count = frames.shape[1]
    chan_count = w_value.shape[1]
    width = col_count * lax.axis_size("col")
    half_width = K // 2
    row_start = lax.axis_index("row") * row_count
    col_start = lax.axis_index("col") * col_count
    local_gain = lax.dynamic_slice_in_dim(gain, col_start, col_count, 0)
    wide = frames.astype(jnp.float32)
    sum_row, square_sum = lax.psum((jnp.sum(wide, axis=1), jnp.sum(wide * wide, axis=1)), "col")
    mean_row = sum_row / width
    inv_std = lax.rsqrt(square_sum / width - mean_row * mean_row + epsilon)
    centred = (wide - mean_row[:, None]) * inv_std[:, None]
    normed = lax.all_gather(
        (centred * local_gain[None, :]).astype(jnp.bfloat16), "col", axis=1, tiled=True
    )
    value_full, gate_full = (
        lax.all_gather(w_value, "row", axis=0, tiled=True),
        lax.all_gather(w_gate, "row", axis=0, tiled=True),
    )
    value_pre = jnp.dot(normed, value_full, preferred_element_type=jnp.float32)
    gate_pre = jnp.dot(normed, gate_full, preferred_element_type=jnp.float32)
    gate_sig = jax.nn.sigmoid(gate_pre)
    gated = (value_pre * gate_sig).astype(jnp.bfloat16)
    padded_glu = extended(gated, (("row", 0),), half_width).astype(jnp.float32)
    local_masks = tap_masks(row_start + jnp.arange(row_count, dtype=jnp.int32))
    conv_pre = jnp.zeros((row_count, chan_count), jnp.float32) + bias[None, :]
    for tap_index in range(K):
        conv_pre = (
            conv_pre
            + kernel[tap_index][None, :]
            * local_masks[tap_index][:, None]
            * padded_glu[tap_index : tap_index + row_count]
        )
    conv_sig = jax.nn.sigmoid(conv_pre)
    activated = (conv_pre * conv_sig).astype(jnp.bfloat16)
    act_full = lax.all_gather(activated, "col", axis=1, tiled=True)
    out_full = lax.all_gather(w_out, "row", axis=0, tiled=True)
    encoded = (
        frames.astype(jnp.float32) + jnp.dot(act_full, out_full, preferred_element_type=jnp.float32)
    ).astype(jnp.bfloat16)
    act_terms = contract_cols(grad_out, out_full)
    act_grad = lax.psum_scatter(
        act_terms.astype(jnp.bfloat16), "col", scatter_dimension=1, tiled=True
    ).astype(jnp.float32)
    grad_out_weight = lax.psum_scatter(
        contract_rows(act_full, grad_out).astype(jnp.bfloat16),
        "row",
        scatter_dimension=0,
        tiled=True,
    ).astype(jnp.float32)
    conv_grad = (act_grad * conv_sig * (1.0 + conv_pre * (1.0 - conv_sig))).astype(jnp.bfloat16)
    conv_wide = conv_grad.astype(jnp.float32)
    padded_grad = extended(conv_grad, (("row", 0),), half_width).astype(jnp.float32)
    outer_masks = tap_masks(
        row_start - half_width + jnp.arange(row_count + 2 * half_width, dtype=jnp.int32)
    )
    glu_grad = jnp.zeros((row_count, chan_count), jnp.float32)
    kernel_rows = []
    for tap_index in range(K):
        begin = 2 * half_width - tap_index
        glu_grad = (
            glu_grad
            + kernel[tap_index][None, :]
            * outer_masks[tap_index, begin : begin + row_count][:, None]
            * padded_grad[begin : begin + row_count]
        )
        kernel_rows.append(
            jnp.sum(
                local_masks[tap_index][:, None]
                * conv_wide
                * padded_glu[tap_index : tap_index + row_count],
                axis=0,
            )
        )
    kernel_term = jnp.stack(kernel_rows)
    bias_term = jnp.sum(conv_wide, axis=0)
    grad_kernel, grad_bias = lax.psum((kernel_term, bias_term), "row")
    value_grad = (glu_grad * gate_sig).astype(jnp.bfloat16)
    gate_grad = (glu_grad * value_pre * gate_sig * (1.0 - gate_sig)).astype(jnp.bfloat16)
    both_grads = jnp.concatenate([value_grad, gate_grad], axis=1)
    in_weight = lax.psum_scatter(
        contract_rows(normed, both_grads).astype(jnp.bfloat16),
        "row",
        scatter_dimension=0,
        tiled=True,
    ).astype(jnp.float32)
    grad_value = in_weight[:, :chan_count]
    grad_gate = in_weight[:, chan_count:]
    norm_terms = contract_cols(value_grad, value_full) + contract_cols(gate_grad, gate_full)
    normed_grad = lax.psum_scatter(
        norm_terms.astype(jnp.bfloat16), "col", scatter_dimension=1, tiled=True
    ).astype(jnp.float32)
    hat_grad = normed_grad * local_gain[None, :]
    first_sum, second_sum = lax.psum(
        (jnp.sum(hat_grad, axis=1), jnp.sum(hat_grad * centred, axis=1)), "col"
    )
    input_grad = (
        grad_out.astype(jnp.float32)
        + inv_std[:, None]
        * (hat_grad - first_sum[:, None] / width - centred * (second_sum / width)[:, None])
    ).astype(jnp.bfloat16)
    gain_term = jnp.sum(normed_grad * centred, axis=0)
    grad_gain = lax.psum(gain_term, "row")
    return (
        encoded,
        input_grad,
        grad_value,
        grad_gate,
        grad_kernel,
        grad_bias,
        grad_out_weight,
        grad_gain,
    )


def solution(mesh):
    placed = (
        P("row", "col"),
        P(),
        P("row", "col"),
        P("row", "col"),
        P(None, "col"),
        P("col"),
        P("row", "col"),
        P("row", "col"),
    )
    return jax.shard_map(
        shards,
        mesh=mesh,
        in_specs=placed,
        out_specs=(
            P("row", "col"),
            P("row", "col"),
            P("row", "col"),
            P("row", "col"),
            P(None, "col"),
            P("col"),
            P("row", "col"),
            P("col"),
        ),
        check_vma=False,
    )
```

profile of v0, /device:TPU:0, one launch (start us, length us, event | category | flops | bytes accessed | tf_op | source)
XLA Modules:
  0.0 864.5 jit_solution(822775014375690964)
XLA Ops:
  7.2 0.7 all-gather.14.cloned.1.call-update
  7.9 0.7 all-gather.10.cloned.1.call-update
  8.7 0.8 dynamic_slice.3
  9.5 1.1 convert_reduce_fusion.1
  10.5 76.2 %all-reduce.1 = (f32[384]{0:T(512)S(1)}, f32[384]{0:T(512)S(1)}) all-reduce(f32[384]{0:T(512)S(1)} %get-tuple-element.44, f32[384]{0:T(512)S(1)} %get-tuple-element.43), channel_id=1, replica_groups=mesh['row'=8,'col'=32] {'col'}, use_global_device_ids=true, to_apply=%region_3.0 | all-reduce | flops 768 | bytes 6144 | tf_op jit(solution)/shard_map/psum | solution.py:52
  86.8 0.6 copy-done.9
  87.3 1.7 fusion.16
  89.1 0.5 all-gather.8.cloned.1.call-update
  89.7 2.3 convolution_convert_fusion
  92.0 2.8 copy.16
  95.0 0.4 copy-done.69
  95.6 0.6 slice_bitcast_fusion.29
  96.2 0.7 slice_bitcast_fusion.30
  96.9 64.5 %all-gather.6.cloned.1.call-done = bf16[384,4096]{1,0:T(8,128)(2,1)} async-done(((bf16[384,128]{1,0:T(8,128)(2,1)}), bf16[384,4096]{1,0:T(8,128)(2,1)}) %all-gather.6.cloned.1.call-update) | async-done | bytes 3145744 | tf_op jit(solution)/shard_map/all_gather | solution.py:56
  161.4 3.3 fusion.2
  164.8 24.6 %all-gather.8.cloned.1.call-done = bf16[4096,128]{1,0:T(8,128)(2,1)} async-done(((bf16[512,128]{1,0:T(8,128)(2,1)}), bf16[4096,128]{1,0:T(8,128)(2,1)}) %all-gather.8.cloned.1.call-update) | async-done | bytes 1048592 | tf_op jit(solution)/shard_map/all_gather | solution.py:60
  189.4 2.9 multiply_convert_fusion.4
  192.3 2.2 collective-permute-start
  194.4 1.3 collective-permute-start.1
  195.9 1.6 collective-permute-done.1
  197.5 215.0 %reduce-scatter.13.cloned.1.call-done = bf16[128,384]{1,0:T(8,128)(2,1)} async-done(((bf16[4096,384]{1,0:T(8,128)(2,1)}), bf16[128,384]{1,0:T(8,128)(2,1)}) %reduce-scatter.13.cloned.1.call-update) | async-done | bytes 98320
  412.5 1.0 copy.17
  414.0 4.1 fusion.75
  418.1 0.7 multiply_convert_fusion.3
  419.2 1.3 collective-permute-start.2
  420.5 1.3 collective-permute-start.3
  421.9 3.3 collective-permute-done.3
  425.6 3.1 multiply_convert_fusion
  428.7 2.6 convolution_convert_fusion.1
  431.4 1.0 fusion.124
  432.7 1.0 add_convert_fusion
  433.6 2.9 copy.18
  436.8 58.9 %all-gather.12.cloned.1.call-done = bf16[384,4096]{1,0:T(8,128)(2,1)} async-done(((bf16[384,128]{1,0:T(8,128)(2,1)}), bf16[384,4096]{1,0:T(8,128)(2,1)}) %all-gather.12.cloned.1.call-update) | async-done | bytes 3145744 | tf_op jit(solution)/shard_map/all_gather | solution.py:79
  495.7 3.9 convolution_convert_fusion.2
  499.7 1.7 fusion.73
  501.4 1.9 fusion.77
  503.3 1.9 fusion.79
  505.1 3.0 stack.127
  508.1 26.7 %reduce-scatter.9.cloned.1.call-done = bf16[512,256]{1,0:T(8,128)(2,1)} async-done(((bf16[4096,256]{1,0:T(8,128)(2,1)}), bf16[512,256]{1,0:T(8,128)(2,1)}) %reduce-scatter.9.cloned.1.call-update) | async-done | bytes 262160 | tf_op jit(solution)/shard_map/reduce_scatter | solution.py:124
  534.8 1.8 fusion.121
  536.6 2.9 fusion.3
  539.5 218.2 %reduce-scatter.15.cloned.1.call-done = bf16[128,384]{1,0:T(8,128)(2,1)} async-done(((bf16[4096,384]{1,0:T(8,128)(2,1)}), bf16[128,384]{1,0:T(8,128)(2,1)}) %reduce-scatter.15.cloned.1.call-update) | async-done | bytes 98320
  757.7 1.0 copy.19
  758.7 0.3 fusion.12
  759.0 72.2 %all-reduce = (f32[384]{0:T(512)S(1)}, f32[384]{0:T(512)S(1)}) all-reduce(f32[384]{0:T(512)S(1)} %get-tuple-element.40, f32[384]{0:T(512)S(1)} %get-tuple-element.41), channel_id=1, replica_groups=mesh['row'=8,'col'=32] {'col'}, use_global_device_ids=true, to_apply=%region_9.10 | all-reduce | flops 768 | bytes 6144 | tf_op jit(solution)/shard_map/psum | solution.py:137
  831.2 24.2 %all-reduce.2 = (f32[31,128]{1,0:T(8,128)}, f32[128]{0:T(128)}, f32[128]{0:T(128)}) all-reduce(f32[31,128]{1,0:T(8,128)S(1)} %stack.127, f32[128]{0:T(128)S(1)} %copy-done.71, f32[128]{0:T(128)S(1)} %get-tuple-element.39), channel_id=1, replica_groups=mesh['row'=8,'col'=32] {'row'}, use_global_device_ids=true, to_apply=%region_42.43 | all-reduce | flops 4224 | bytes 33792 | tf_op jit(solution)/shard_map/psum | solution.py:120
  855.4 0.9 fusion.10
  856.3 1.6 convert_element_type.92
  (178 shorter events, 2.0 us)
Async XLA Ops:
  7.2 82.6 %all-gather.14.cloned.1.call-start = ((), (), s32[]{:S(2)}) async-start(), calls=%async_computation.8 | async-start | bytes 1179648 | tf_op jit(solution)/shard_map/all_gather | solution.py:80
  7.9 89.0 %all-gather.10.cloned.1.call-start = ((), (), s32[]{:S(2)}) async-start(), calls=%async_computation.6 | async-start | bytes 1179648 | tf_op jit(solution)/shard_map/all_gather | solution.py:61
  8.7 152.8 %all-gather.6.cloned.1.call-start = ((), (), s32[]{:S(2)}) async-start(), calls=%async_computation.4 | async-start | bytes 3244032 | tf_op jit(solution)/shard_map/all_gather | solution.py:56
  9.5 80.2 %copy-start.36 = (f32[128]{0:T(128)}, f32[128]{0:T(128)S(1)}, u32[]{:S(2)}) copy-start(f32[128]{0:T(128)S(1)} %dynamic_slice.3) | copy-start | bytes 1540
  89.1 100.3 %all-gather.8.cloned.1.call-start = ((), (), s32[]{:S(2)}) async-start(), calls=%async_computation.5 | async-start | bytes 1179648 | tf_op jit(solution)/shard_map/all_gather | solution.py:60
  89.6 322.9 %reduce-scatter.13.cloned.1.call-start = ((), (), s32[]{:S(2)}) async-start(), calls=%async_computation.11 | async-start | bytes 3244032
  94.8 400.9 %all-gather.12.cloned.1.call-start = ((), (), s32[]{:S(2)}) async-start(), calls=%async_computation.7 | async-start | bytes 3244032 | tf_op jit(solution)/shard_map/all_gather | solution.py:79
  95.5 318.0 %copy-start.13 = (f32[384]{0:T(512)}, f32[384]{0:T(512)S(1)}, u32[]{:S(2)}) copy-start(f32[384]{0:T(512)S(1)} %get-tuple-element.77) | copy-start | bytes 4612
  95.5 318.0 %copy-start.14 = (f32[384]{0:T(512)}, f32[384]{0:T(512)S(1)}, u32[]{:S(2)}) copy-start(f32[384]{0:T(512)S(1)} %get-tuple-element.78) | copy-start | bytes 4612
  95.5 318.0 %copy-start.15 = (f32[384]{0:T(512)}, f32[384]{0:T(512)S(1)}, u32[]{:S(2)}) copy-start(f32[384]{0:T(512)S(1)} %get-tuple-element.91) | copy-start | bytes 4612
  95.5 318.0 %copy-start.16 = (f32[384]{0:T(512)}, f32[384]{0:T(512)S(1)}, u32[]{:S(2)}) copy-start(f32[384]{0:T(512)S(1)} %get-tuple-element.92) | copy-start | bytes 4612
  95.5 318.0 %copy-start.17 = (f32[384]{0:T(512)}, f32[384]{0:T(512)S(1)}, u32[]{:S(2)}) copy-start(f32[384]{0:T(512)S(1)} %get-tuple-element.93) | copy-start | bytes 4612
  95.5 318.0 %copy-start.18 = (f32[384]{0:T(512)}, f32[384]{0:T(512)S(1)}, u32[]{:S(2)}) copy-start(f32[384]{0:T(512)S(1)} %get-tuple-element.94) | copy-start | bytes 4612
  95.5 318.0 %copy-start.19 = (f32[384]{0:T(512)}, f32[384]{0:T(512)S(1)}, u32[]{:S(2)}) copy-start(f32[384]{0:T(512)S(1)} %get-tuple-element.76) | copy-start | bytes 4612
  95.6 318.0 %copy-start.20 = (f32[384]{0:T(512)}, f32[384]{0:T(512)S(1)}, u32[]{:S(2)}) copy-start(f32[384]{0:T(512)S(1)} %get-tuple-element.80) | copy-start | bytes 4612
  95.6 318.0 %copy-start.21 = (f32[384]{0:T(512)}, f32[384]{0:T(512)S(1)}, u32[]{:S(2)}) copy-start(f32[384]{0:T(512)S(1)} %get-tuple-element.81) | copy-start | bytes 4612
  95.6 318.0 %copy-start.22 = (f32[384]{0:T(512)}, f32[384]{0:T(512)S(1)}, u32[]{:S(2)}) copy-start(f32[384]{0:T(512)S(1)} %get-tuple-element.82) | copy-start | bytes 4612
  96.2 317.4 %copy-start.38 = (f32[128]{0:T(128)}, f32[128]{0:T(128)S(1)}, u32[]{:S(2)}) copy-start(f32[128]{0:T(128)S(1)} %get-tuple-element.143) | copy-start | bytes 1540
  96.2 317.4 %copy-start.39 = (f32[128]{0:T(128)}, f32[128]{0:T(128)S(1)}, u32[]{:S(2)}) copy-start(f32[128]{0:T(128)S(1)} %get-tuple-element.144) | copy-start | bytes 1540
  96.2 317.4 %copy-start.40 = (f32[128]{0:T(128)}, f32[128]{0:T(128)S(1)}, u32[]{:S(2)}) copy-start(f32[128]{0:T(128)S(1)} %get-tuple-element.145) | copy-start | bytes 1540
  96.2 317.4 %copy-start.41 = (f32[128]{0:T(128)}, f32[128]{0:T(128)S(1)}, u32[]{:S(2)}) copy-start(f32[128]{0:T(128)S(1)} %get-tuple-element.146) | copy-start | bytes 1540
  96.2 317.4 %copy-start.42 = (f32[128]{0:T(128)}, f32[128]{0:T(128)S(1)}, u32[]{:S(2)}) copy-start(f32[128]{0:T(128)S(1)} %get-tuple-element.147) | copy-start | bytes 1540
  192.3 3.7 collective-permute-start
  194.4 3.1 collective-permute-start.1
  195.8 222.2 %copy-start.23 = (f32[384]{0:T(512)}, f32[384]{0:T(512)S(1)}, u32[]{:S(2)}) copy-start(f32[384]{0:T(512)S(1)} %get-tuple-element.95) | copy-start | bytes 4612
  195.8 222.2 %copy-start.24 = (f32[384]{0:T(512)}, f32[384]{0:T(512)S(1)}, u32[]{:S(2)}) copy-start(f32[384]{0:T(512)S(1)} %get-tuple-element.100) | copy-start | bytes 4612
  195.8 222.2 %copy-start.25 = (f32[384]{0:T(512)}, f32[384]{0:T(512)S(1)}, u32[]{:S(2)}) copy-start(f32[384]{0:T(512)S(1)} %get-tuple-element.101) | copy-start | bytes 4612
  195.8 222.2 %copy-start.26 = (f32[384]{0:T(512)}, f32[384]{0:T(512)S(1)}, u32[]{:S(2)}) copy-start(f32[384]{0:T(512)S(1)} %get-tuple-element.102) | copy-start | bytes 4612
  195.8 222.2 %copy-start.27 = (f32[384]{0:T(512)}, f32[384]{0:T(512)S(1)}, u32[]{:S(2)}) copy-start(f32[384]{0:T(512)S(1)} %get-tuple-element.103) | copy-start | bytes 4612
  195.8 222.2 %copy-start.28 = (f32[384]{0:T(512)}, f32[384]{0:T(512)S(1)}, u32[]{:S(2)}) copy-start(f32[384]{0:T(512)S(1)} %get-tuple-element.104) | copy-start | bytes 4612
  195.8 222.2 %copy-start.29 = (f32[384]{0:T(512)}, f32[384]{0:T(512)S(1)}, u32[]{:S(2)}) copy-start(f32[384]{0:T(512)S(1)} %get-tuple-element.105) | copy-start | bytes 4612
  195.9 222.2 %copy-start.30 = (f32[384]{0:T(512)}, f32[384]{0:T(512)S(1)}, u32[]{:S(2)}) copy-start(f32[384]{0:T(512)S(1)} %get-tuple-element.106) | copy-start | bytes 4612
  195.9 222.2 %copy-start.31 = (f32[384]{0:T(512)}, f32[384]{0:T(512)S(1)}, u32[]{:S(2)}) copy-start(f32[384]{0:T(512)S(1)} %get-tuple-element.96) | copy-start | bytes 4612
  195.9 222.2 %copy-start.32 = (f32[384]{0:T(512)}, f32[384]{0:T(512)S(1)}, u32[]{:S(2)}) copy-start(f32[384]{0:T(512)S(1)} %get-tuple-element.97) | copy-start | bytes 4612
  195.9 222.2 %copy-start.33 = (f32[384]{0:T(512)}, f32[384]{0:T(512)S(1)}, u32[]{:S(2)}) copy-start(f32[384]{0:T(512)S(1)} %get-tuple-element.98) | copy-start | bytes 4612
  195.9 222.2 %copy-start.34 = (f32[384]{0:T(512)}, f32[384]{0:T(512)S(1)}, u32[]{:S(2)}) copy-start(f32[384]{0:T(512)S(1)} %get-tuple-element.99) | copy-start | bytes 4612
  418.9 116.0 %reduce-scatter.9.cloned.1.call-start = ((), (), s32[]{:S(2)}) async-start(), calls=%async_computation.9 | async-start | bytes 2359296 | tf_op jit(solution)/shard_map/reduce_scatter | solution.py:124
  419.2 2.7 collective-permute-start.2
  420.5 4.8 collective-permute-start.3
  431.4 326.3 %reduce-scatter.15.cloned.1.call-start = ((), (), s32[]{:S(2)}) async-start(), calls=%async_computation.12 | async-start | bytes 3244032
  436.5 59.2 %copy-start.6 = (bf16[384,128]{1,0:T(8,128)(2,1)S(1)}, bf16[384,128]{1,0:T(8,128)(2,1)}, u32[]{:S(2)}) copy-start(bf16[384,128]{1,0:T(8,128)(2,1)} %param.15) | copy-start | bytes 294916
  436.6 419.8 %reduce-scatter.11.cloned.1.call-start = ((), (), s32[]{:S(2)}) async-start(), calls=%async_computation.10 | async-start | bytes 1179648 | tf_op jit(solution)/shard_map/reduce_scatter | solution.py:88
  499.6 37.0 %copy-start = (bf16[384,4096]{1,0:T(8,128)(2,1)S(1)}, bf16[384,4096]{1,0:T(8,128)(2,1)}, u32[]{:S(2)}) copy-start(bf16[384,4096]{1,0:T(8,128)(2,1)} %all-gather.12.cloned.1.call-done) | copy-start | bytes 9437188
  505.1 253.6 %copy-start.10 = (f32[384]{0:T(512)S(1)}, f32[384]{0:T(512)}, u32[]{:S(2)}) copy-start(f32[384]{0:T(512)} %copy-done.9) | copy-start | bytes 4612
  505.1 253.6 %copy-start.12 = (f32[384]{0:T(512)S(1)}, f32[384]{0:T(512)}, u32[]{:S(2)}) copy-start(f32[384]{0:T(512)} %copy-done.11) | copy-start | bytes 4612
  505.1 253.6 %copy-start.37 = (f32[128]{0:T(128)S(1)}, f32[128]{0:T(128)}, u32[]{:S(2)}) copy-start(f32[128]{0:T(128)} %copy-done.36) | copy-start | bytes 1540
  505.1 326.1 %copy-start.71 = (f32[128]{0:T(128)S(1)}, f32[128]{0:T(128)}, u32[]{:S(2)}) copy-start(f32[128]{0:T(128)} %get-tuple-element.42) | copy-start | bytes 1540
  505.1 350.3 %copy-start.7 = (bf16[384,128]{1,0:T(8,128)(2,1)S(1)}, bf16[384,128]{1,0:T(8,128)(2,1)}, u32[]{:S(2)}) copy-start(bf16[384,128]{1,0:T(8,128)(2,1)} %param.15) | copy-start | bytes 294916
  (37 other events, 393.1 us)
Sparse Core Ops, SparseCore 0:
  9.9 27.1 all-gather.13
  38.9 25.7 all-gather.9
  89.2 72.2 all-gather.5
  163.2 26.1 all-gather.7
  193.1 219.3 reduce-scatter.12
  419.0 76.6 all-gather.11
  498.4 36.3 reduce-scatter.8
  539.2 218.4 reduce-scatter.14
  760.2 32.8 reduce-scatter.10
where the time goes:
time: 865 us; the launch traced here: 864 us
  waiting for transfers between devices  615 us (71%)
  blocking collectives  173 us (20%)
  matrix products  19.8 us (2%)
  other arithmetic  19.2 us (2%)
  local copies, waits for them, and re-layouts  16.5 us (2%)
  between operations  15 us (2%)
    unnamed x11, waiting for transfers between devices  435 us
    psum x1, blocking collectives, shards(): lax.psum((jnp.sum(wide, axis=1), jnp.sum(wide * wide, axis=1)), 'col')  76.2 us
    psum x1, blocking collectives, shards(): lax.psum((jnp.sum(hat_grad, axis=1), jnp.sum(hat_grad * centred, axis=1))...  72.2 us
    all_gather x1, waiting for transfers between devices, shards(): lax.all_gather((centred * local_gain[None, :]).astype(jnp.bfloat16), 'col...  64.5 us
    all_gather x1, waiting for transfers between devices, shards(): act_full = lax.all_gather(activated, 'col', axis=1, tiled=True)  58.9 us
    reduce_scatter x1, waiting for transfers between devices, shards(): lax.psum_scatter(contract_rows(normed, both_grads).astype(jnp.bfloat16),...  26.7 us
    all_gather x1, waiting for transfers between devices, shards(): lax.all_gather(w_value, 'row', axis=0, tiled=True)  24.6 us
    psum x1, blocking collectives, shards(): grad_kernel, grad_bias = lax.psum((kernel_term, bias_term), 'row')  24.2 us
  transfers between devices with their start and end apart: 13, of which 8 were waited for; matrix products, arithmetic and copies ran while one was open for 5% of the time, Pallas kernels for 0%

commit v1 on v0

--- a/solution.py
+++ b/solution.py
@@ -6,6 +6,19 @@
 K = 31
 LEN = 2048
 epsilon = 1e-05
+
+
+def gather_around(x, axis, dim):
+    ways = lax.axis_size(axis)
+    up = [(d, (d + 1) % ways) for d in range(ways)]
+    down = [(d, (d - 1) % ways) for d in range(ways)]
+    earlier, later = ([x], [x])
+    for _ in range(ways // 2):
+        earlier.append(lax.ppermute(earlier[-1], axis, up))
+    for _ in range((ways - 1) // 2):
+        later.append(lax.ppermute(later[-1], axis, down))
+    line = jnp.concatenate([*earlier[::-1], *later[1:]], axis=dim)
+    return jnp.roll(line, (lax.axis_index(axis) - ways // 2) * x.shape[dim], axis=dim)
 
 
 def extended(block, sides, width):
@@ -57,7 +70,7 @@
         (centred * local_gain[None, :]).astype(jnp.bfloat16), "col", axis=1, tiled=True
     )
     value_full, gate_full = (
-        lax.all_gather(w_value, "row", axis=0, tiled=True),
+        gather_around(w_value, "row", 0),
         lax.all_gather(w_gate, "row", axis=0, tiled=True),
     )
     value_pre = jnp.dot(normed, value_full, preferred_element_type=jnp.float32)

time: 865 us -> 837 us (0.968)
  waiting for transfers between devices: 615 us -> 563 us
  local copies, waits for them, and re-layouts: 16.5 us -> 29.8 us
    all_gather x1, waiting for transfers between devices: 64.5 us -> 33.3 us  [shards(): lax.all_gather((centred * local_gain[None, :]).astype(jnp.bfloat16), 'col...]
    all_gather x1 -> x0, waiting for transfers between devices: 24.6 us -> none  [shards(): lax.all_gather(w_value, 'row', axis=0, tiled=True)]
    unnamed x148 -> x69, local copies, waits for them, and re-layouts: 9.21 us -> 20.8 us
    ppermute x0 -> x7, waiting for transfers between devices: none -> 11.4 us  [the longest x4 11.4 us: gather_around(): earlier.append(lax.ppermute(earlier[-1], axis, up))]
    ppermute x0 -> x7, starting transfers between devices: none -> 8.88 us  [the longest x3 8.87 us: gather_around(): later.append(lax.ppermute(later[-1], axis, down))]
    unnamed x11 -> x10, waiting for transfers between devices: 435 us -> 430 us
  transfers between devices with their start and end apart: 13 -> 19, of which waited for: 8 -> 11; matrix products, arithmetic and copies ran while one was open for 5% -> 7% of each run, Pallas kernels for 0% -> 0%
where the time goes in v1:
time: 837 us; the launch traced here: 836 us
  waiting for transfers between devices  563 us (67%)
  blocking collectives  173 us (21%)
  local copies, waits for them, and re-layouts  29.8 us (4%)
  matrix products  21.2 us (3%)
  other arithmetic  20.4 us (2%)
  starting transfers between devices  14.5 us (2%)
  between operations  14.5 us (2%)
    unnamed x10, waiting for transfers between devices  430 us
    psum x1, blocking collectives, shards(): lax.psum((jnp.sum(wide, axis=1), jnp.sum(wide * wide, axis=1)), 'col')  76.2 us
    psum x1, blocking collectives, shards(): lax.psum((jnp.sum(hat_grad, axis=1), jnp.sum(hat_grad * centred, axis=1))...  72.2 us
    all_gather x1, waiting for transfers between devices, shards(): act_full = lax.all_gather(activated, 'col', axis=1, tiled=True)  55.4 us
    all_gather x1, waiting for transfers between devices, shards(): lax.all_gather((centred * local_gain[None, :]).astype(jnp.bfloat16), 'col...  33.3 us
    reduce_scatter x1, waiting for transfers between devices, shards(): lax.psum_scatter(contract_rows(normed, both_grads).astype(jnp.bfloat16),...  27.3 us
    psum x1, blocking collectives, shards(): grad_kernel, grad_bias = lax.psum((kernel_term, bias_term), 'row')  24.2 us
    unnamed x69, local copies, waits for them, and re-layouts  20.8 us
  transfers between devices with their start and end apart: 19, of which 11 were waited for; matrix products, arithmetic and copies ran while one was open for 7% of the time, Pallas kernels for 0%

profile of v1, /device:TPU:0, one launch (start us, length us, event | category | flops | bytes accessed | tf_op | source)
XLA Modules:
  0.0 836.2 jit_solution(8200797047735621637)
XLA Ops:
  8.7 0.8 dynamic_slice.7
  9.5 1.1 convert_reduce_fusion.1
  10.5 76.2 %all-reduce.1 = (f32[384]{0:T(512)S(1)}, f32[384]{0:T(512)S(1)}) all-reduce(f32[384]{0:T(512)S(1)} %get-tuple-element.44, f32[384]{0:T(512)S(1)} %get-tuple-element.43), channel_id=1, replica_groups=mesh['row'=8,'col'=32] {'col'}, use_global_device_ids=true, to_apply=%region_3.0 | all-reduce | flops 768 | bytes 6144 | tf_op jit(solution)/shard_map/psum | solution.py:65
  87.3 1.7 fusion.19
  89.2 2.3 convolution_convert_fusion
  91.4 2.8 copy.16
  94.3 0.8 copy-done.9
  95.2 3.0 collective-permute-start.4
  98.1 2.6 collective-permute-done
  100.9 5.5 collective-permute-done.1
  107.0 3.0 collective-permute-start.5
  110.0 2.0 collective-permute-done.2
  113.3 3.0 collective-permute-start.6
  116.2 1.3 collective-permute-done.3
  128.1 33.3 %all-gather.5.cloned.1.call-done = bf16[384,4096]{1,0:T(8,128)(2,1)} async-done(((bf16[384,128]{1,0:T(8,128)(2,1)}), bf16[384,4096]{1,0:T(8,128)(2,1)}) %all-gather.5.cloned.1.call-update) | async-done | bytes 3145744 | tf_op jit(solution)/shard_map/all_gather | solution.py:69
  161.4 3.3 fusion.2
  164.8 3.0 multiply_convert_fusion.4
  167.7 1.3 collective-permute-start.7
  169.0 1.3 collective-permute-start.8
  171.0 2.8 collective-permute-done.8
  173.8 210.1 %reduce-scatter.13.cloned.1.call-done = bf16[128,384]{1,0:T(8,128)(2,1)} async-done(((bf16[4096,384]{1,0:T(8,128)(2,1)}), bf16[128,384]{1,0:T(8,128)(2,1)}) %reduce-scatter.13.cloned.1.call-update) | async-done | bytes 98320
  384.0 1.0 copy.17
  385.0 4.9 fusion.78
  390.7 0.8 fusion.117
  391.6 1.3 collective-permute-start.9
  392.9 1.3 collective-permute-start.10
  394.4 3.3 collective-permute-done.10
  397.7 3.5 multiply_convert_fusion.1
  401.9 2.6 convolution_convert_fusion.1
  404.6 1.1 copy-done.5
  405.7 1.0 fusion.129
  406.7 2.2 add_convert_fusion
  408.9 2.8 copy.18
  412.1 55.4 %all-gather.9.cloned.1.call-done = bf16[384,4096]{1,0:T(8,128)(2,1)} async-done(((bf16[384,128]{1,0:T(8,128)(2,1)}), bf16[384,4096]{1,0:T(8,128)(2,1)}) %all-gather.9.cloned.1.call-update) | async-done | bytes 3145744 | tf_op jit(solution)/shard_map/all_gather | solution.py:92
  467.5 4.0 convolution_convert_fusion.2
  471.5 0.8 fusion.76
  472.3 2.0 fusion.80
  474.3 1.9 fusion.82
  476.2 2.9 stack.127
  479.1 27.3 %reduce-scatter.9.cloned.1.call-done = bf16[512,256]{1,0:T(8,128)(2,1)} async-done(((bf16[4096,256]{1,0:T(8,128)(2,1)}), bf16[512,256]{1,0:T(8,128)(2,1)}) %reduce-scatter.9.cloned.1.call-update) | async-done | bytes 262160 | tf_op jit(solution)/shard_map/reduce_scatter | solution.py:137
  506.5 1.8 fusion.126
  508.3 2.9 fusion.3
  511.2 218.0 %reduce-scatter.15.cloned.1.call-done = bf16[128,384]{1,0:T(8,128)(2,1)} async-done(((bf16[4096,384]{1,0:T(8,128)(2,1)}), bf16[128,384]{1,0:T(8,128)(2,1)}) %reduce-scatter.15.cloned.1.call-update) | async-done | bytes 98320
  729.2 1.0 copy.19
  730.5 72.2 %all-reduce = (f32[384]{0:T(512)S(1)}, f32[384]{0:T(512)S(1)}) all-reduce(f32[384]{0:T(512)S(1)} %get-tuple-element.40, f32[384]{0:T(512)S(1)} %get-tuple-element.41), channel_id=1, replica_groups=mesh['row'=8,'col'=32] {'col'}, use_global_device_ids=true, to_apply=%region_9.10 | all-reduce | flops 768 | bytes 6144 | tf_op jit(solution)/shard_map/psum | solution.py:150
  802.7 24.2 %all-reduce.2 = (f32[31,128]{1,0:T(8,128)}, f32[128]{0:T(128)}, f32[128]{0:T(128)}) all-reduce(f32[31,128]{1,0:T(8,128)S(1)} %stack.127, f32[128]{0:T(128)S(1)} %copy-done.24, f32[128]{0:T(128)S(1)} %get-tuple-element.39), channel_id=1, replica_groups=mesh['row'=8,'col'=32] {'row'}, use_global_device_ids=true, to_apply=%region_42.43 | all-reduce | flops 4224 | bytes 33792 | tf_op jit(solution)/shard_map/psum | solution.py:133
  826.8 0.9 fusion.13
  827.8 1.6 convert_element_type.92
  (111 shorter events, 18.0 us)
Async XLA Ops:
  7.2 82.0 %all-gather.11.cloned.1.call-start = ((), (), s32[]{:S(2)}) async-start(), calls=%async_computation.7 | async-start | bytes 1179648 | tf_op jit(solution)/shard_map/all_gather | solution.py:93
  7.9 120.2 %all-gather.7.cloned.1.call-start = ((), (), s32[]{:S(2)}) async-start(), calls=%async_computation.5 | async-start | bytes 1179648 | tf_op jit(solution)/shard_map/all_gather | solution.py:74
  8.7 152.8 %all-gather.5.cloned.1.call-start = ((), (), s32[]{:S(2)}) async-start(), calls=%async_computation.4 | async-start | bytes 3244032 | tf_op jit(solution)/shard_map/all_gather | solution.py:69
  9.5 79.7 %copy-start.21 = (f32[128]{0:T(128)}, f32[128]{0:T(128)S(1)}, u32[]{:S(2)}) copy-start(f32[128]{0:T(128)S(1)} %dynamic_slice.7) | copy-start | bytes 1540
  86.7 0.6 copy-start.12
  86.7 0.6 copy-start.14
  89.1 294.9 %reduce-scatter.13.cloned.1.call-start = ((), (), s32[]{:S(2)}) async-start(), calls=%async_computation.10 | async-start | bytes 3244032
  94.2 0.9 copy-start.9
  94.2 12.1 %copy-start.20 = (f32[31,128]{1,0:T(8,128)S(1)}, f32[31,128]{1,0:T(8,128)}, u32[]{:S(2)}) copy-start(f32[31,128]{1,0:T(8,128)} %param.12) | copy-start | bytes 47620
  94.3 373.2 %all-gather.9.cloned.1.call-start = ((), (), s32[]{:S(2)}) async-start(), calls=%async_computation.6 | async-start | bytes 3244032 | tf_op jit(solution)/shard_map/all_gather | solution.py:92
  95.2 5.6 collective-permute-start
  95.2 11.9 %collective-permute-start.4 = (bf16[512,128]{1,0:T(8,128)(2,1)S(1)}, bf16[512,128]{1,0:T(8,128)(2,1)S(1)}, u32[]{:S(2)}, u32[]{:S(2)}) collective-permute-start(bf16[512,128]{1,0:T(8,128)(2,1)S(1)} %copy-done.9), channel_id=1, source_target_pairs={{0,224},{32,0},{64,32},{96,64},{128,96},{160,128},{192,160},{224,1... | collective-permute-start | bytes 393224 | tf_op jit(solution)/shard_map/ppermute | solution.py:19
  98.1 2.7 copy-start.23
  100.8 5.6 collective-permute-start.1
  106.4 5.6 collective-permute-start.2
  107.0 6.2 collective-permute-start.5
  112.0 5.6 collective-permute-start.3
  113.3 8.9 %collective-permute-start.6 = (bf16[512,128]{1,0:T(8,128)(2,1)S(1)}, bf16[512,128]{1,0:T(8,128)(2,1)S(1)}, u32[]{:S(2)}, u32[]{:S(2)}) collective-permute-start(bf16[512,128]{1,0:T(8,128)(2,1)S(1)} %collective-permute-done.5), channel_id=1, source_target_pairs={{0,224},{32,0},{64,32},{96,64},{128,96},{160,128},{192,160},{224,1... | collective-permute-start | bytes 393224 | tf_op jit(solution)/shard_map/ppermute | solution.py:19
  161.4 3.3 copy-start.1
  164.8 6.2 copy-start.3
  167.7 3.3 collective-permute-start.7
  169.0 4.8 collective-permute-start.8
  390.6 115.8 %reduce-scatter.9.cloned.1.call-start = ((), (), s32[]{:S(2)}) async-start(), calls=%async_computation.8 | async-start | bytes 2359296 | tf_op jit(solution)/shard_map/reduce_scatter | solution.py:137
  391.6 2.7 collective-permute-start.9
  392.9 4.7 collective-permute-start.10
  397.7 3.5 copy-start.4
  397.7 3.5 copy-start.8
  401.2 0.6 copy-start.10
  404.5 1.2 copy-start.5
  404.5 324.6 %reduce-scatter.15.cloned.1.call-start = ((), (), s32[]{:S(2)}) async-start(), calls=%async_computation.11 | async-start | bytes 3244032
  405.7 1.0 copy-start.11
  411.8 55.7 %copy-start.6 = (bf16[384,128]{1,0:T(8,128)(2,1)S(1)}, bf16[384,128]{1,0:T(8,128)(2,1)}, u32[]{:S(2)}) copy-start(bf16[384,128]{1,0:T(8,128)(2,1)} %param.15) | copy-start | bytes 294916
  411.8 59.7 %copy-start.16 = (f32[384]{0:T(512)S(1)}, f32[384]{0:T(512)}, u32[]{:S(2)}) copy-start(f32[384]{0:T(512)} %get-tuple-element.76) | copy-start | bytes 4612
  411.8 59.6 %copy-start.17 = (f32[384]{0:T(512)S(1)}, f32[384]{0:T(512)}, u32[]{:S(2)}) copy-start(f32[384]{0:T(512)} %get-tuple-element.80) | copy-start | bytes 4612
  411.8 59.6 %copy-start.18 = (f32[384]{0:T(512)S(1)}, f32[384]{0:T(512)}, u32[]{:S(2)}) copy-start(f32[384]{0:T(512)} %get-tuple-element.81) | copy-start | bytes 4612
  411.8 59.6 %copy-start.19 = (f32[384]{0:T(512)S(1)}, f32[384]{0:T(512)}, u32[]{:S(2)}) copy-start(f32[384]{0:T(512)} %get-tuple-element.82) | copy-start | bytes 4612
  411.8 415.9 %reduce-scatter.11.cloned.1.call-start = ((), (), s32[]{:S(2)}) async-start(), calls=%async_computation.9 | async-start | bytes 1179648 | tf_op jit(solution)/shard_map/reduce_scatter | solution.py:101
  472.3 36.0 %copy-start = (bf16[384,4096]{1,0:T(8,128)(2,1)S(1)}, bf16[384,4096]{1,0:T(8,128)(2,1)}, u32[]{:S(2)}) copy-start(bf16[384,4096]{1,0:T(8,128)(2,1)} %all-gather.9.cloned.1.call-done) | copy-start | bytes 9437188
  472.3 36.0 %copy-start.2 = (bf16[384,128]{1,0:T(8,128)(2,1)S(1)}, bf16[384,128]{1,0:T(8,128)(2,1)}, u32[]{:S(2)}) copy-start(bf16[384,128]{1,0:T(8,128)(2,1)} %param.8) | copy-start | bytes 294916
  508.3 221.9 %copy-start.13 = (f32[384]{0:T(512)S(1)}, f32[384]{0:T(512)}, u32[]{:S(2)}) copy-start(f32[384]{0:T(512)} %copy-done.12) | copy-start | bytes 4612
  508.3 221.9 %copy-start.15 = (f32[384]{0:T(512)S(1)}, f32[384]{0:T(512)}, u32[]{:S(2)}) copy-start(f32[384]{0:T(512)} %copy-done.14) | copy-start | bytes 4612
  508.3 221.9 %copy-start.22 = (f32[128]{0:T(128)S(1)}, f32[128]{0:T(128)}, u32[]{:S(2)}) copy-start(f32[128]{0:T(128)} %copy-done.21) | copy-start | bytes 1540
  508.3 294.4 %copy-start.24 = (f32[128]{0:T(128)S(1)}, f32[128]{0:T(128)}, u32[]{:S(2)}) copy-start(f32[128]{0:T(128)} %get-tuple-element.42) | copy-start | bytes 1540
  508.3 318.5 %copy-start.7 = (bf16[384,128]{1,0:T(8,128)(2,1)S(1)}, bf16[384,128]{1,0:T(8,128)(2,1)}, u32[]{:S(2)}) copy-start(bf16[384,128]{1,0:T(8,128)(2,1)} %param.15) | copy-start | bytes 294916
Sparse Core Ops, SparseCore 0:
  9.9 27.1 all-gather.10
  38.9 25.7 all-gather.6
  89.2 72.2 all-gather.4
  165.2 218.7 reduce-scatter.12
  390.8 76.6 all-gather.8
  470.0 36.3 reduce-scatter.8
  510.8 218.2 reduce-scatter.14
  731.7 32.9 reduce-scatter.10
